TPU v7x, 32 devices: a whole 2x2x4 slice. The times are simulated.
32 devices in a mesh: row: 4 (over x, core), col: 8 (over z, y).
Axes of the slice: x: 2, y: 2, z: 4, core: 2. Of those that a mesh axis runs over, the one named last changes fastest.
Arguments:
- pair_density: bfloat16 [2048, 8192], P('col', 'row'), may hold values from -6 to 6
- scale_exp: int32 [2048], replicated, may hold values from -1 to 1
- pair_weight: int32 [2048], replicated, may hold values from 1 to 4
- resident_ids: int32 [512], replicated, may hold values from 0 to 2047, as said below
- diagonal_shift: float32 [8192], replicated, may hold values from 2 to 4
- background: float32 [8192, 8192], P('row', 'col'), as said below
Outputs:
- dielectric: float32 [8192, 8192], P('row', 'col')
- kernel: float32 [2048, 512], P(('col', 'row'))
Inputs may be any that keep to these rules, and one draw needn't show every extreme that they name: `resident_ids`: 512 distinct pair indices. background is symmetric.
All inputs are finite; a program needn't handle non-finite values.
Results may differ from a plain program's by a relative error of at most 0.0003.
Values may be sent and summed in bfloat16 or wider, within the bound.
No kernel may reach another device: no remote copies, remote signals or barrier semaphores. Data moves between devices by JAX's collectives and lax.ppermute only.
A program may use at most 128 MiB of HBM per device.

v0:
```python
import math
import jax
import jax.numpy as jnp
from jax import lax
from jax.sharding import PartitionSpec as P

NG = 8192
SWEEPS = 2
damping = 0.5


def from_root(block, axis, owner):
    block = jnp.where(lax.axis_index(axis) == owner, block, jnp.zeros_like(block))
    return lax.psum(block, axis)


def scale_factor(exponent):
    return jnp.where(exponent < 0, 0.5, jnp.where(exponent > 0, 2.0, 1.0)).astype(jnp.float32)


def pair_contract(left_block, right_block):
    return lax.dot_general(
        left_block, right_block, (((0,), (0,)), ((), ())), preferred_element_type=jnp.float32
    )


def shards(pair_density, scale_exp, pair_weight, resident_ids, diagonal_shift, background):
    row_count = lax.axis_size("row")
    col_count = lax.axis_size("col")
    row_index = lax.axis_index("row")
    col_index = lax.axis_index("col")
    pair_dev, row_width = pair_density.shape
    col_width = background.shape[1]
    pair_total = pair_dev * col_count
    norm_scale = 4 * pair_total
    factor = scale_factor(scale_exp)
    own_factor = lax.dynamic_slice_in_dim(factor, col_index * pair_dev, pair_dev)
    scaled = (pair_density.astype(jnp.float32) * own_factor[:, None]).astype(jnp.bfloat16)
    left_all = lax.all_gather(scaled, "col", axis=0, tiled=True)
    relaid = lax.all_to_all(
        lax.all_to_all(scaled, "row", split_axis=0, concat_axis=1, tiled=True),
        "col",
        split_axis=1,
        concat_axis=0,
        tiled=True,
    )
    share_rows = pair_dev // row_count
    left_order = left_all.reshape(col_count, row_count, share_rows, row_width)
    left_order = left_order.transpose(1, 0, 2, 3).reshape(pair_total, row_width)
    contracted = pair_contract(left_order, lax.all_gather(relaid, "row", axis=0, tiled=True))
    response = contracted / norm_scale
    row_start = row_index * row_width
    col_start = col_index * col_width
    global_rows = row_start + lax.broadcasted_iota(jnp.int32, (row_width, col_width), 0)
    global_cols = col_start + lax.broadcasted_iota(jnp.int32, (row_width, col_width), 1)
    shift_rows = lax.dynamic_slice_in_dim(diagonal_shift, row_start, row_width)
    dielectric = (
        background + response + jnp.where(global_rows == global_cols, shift_rows[:, None], 0.0)
    )
    precond_rows = (
        shift_rows
        + jnp.einsum("pg,pg->g", left_all, left_all, preferred_element_type=jnp.float32)
        / norm_scale
    )
    picked = left_all[resident_ids].astype(jnp.float32) / factor[resident_ids][:, None]
    source_rows = picked.T
    col_ratio = col_count // row_count
    root_row = col_index // col_ratio
    offset = col_index % col_ratio * col_width

    def column_share(values):
        return lax.dynamic_slice_in_dim(values, offset, col_width, 0)

    source_cols, precond_cols = (
        from_root(column_share(source_rows), "row", root_row),
        from_root(column_share(precond_rows), "row", root_row),
    )
    screen_rows = source_rows / precond_rows[:, None]
    screen_cols = source_cols / precond_cols[:, None]
    for sweep_index in range(SWEEPS):
        last_sweep = sweep_index + 1 == SWEEPS
        row_image = lax.psum(
            jnp.dot(dielectric, screen_cols, precision=lax.Precision.HIGHEST), "col"
        )
        if not last_sweep:
            transposed = lax.dot_general(
                dielectric, screen_rows, (((0,), (0,)), ((), ())), precision=lax.Precision.HIGHEST
            )
            col_image = lax.psum(transposed, "row")
            screen_cols = screen_cols + damping * (source_cols - col_image) / precond_cols[:, None]
        screen_rows = screen_rows + damping * (source_rows - row_image) / precond_rows[:, None]
    partial_value = jnp.dot(
        pair_density.astype(jnp.float32), screen_rows, precision=lax.Precision.HIGHEST
    )
    summed = lax.psum_scatter(partial_value, "row", scatter_dimension=0, tiled=True)
    kernel_share = pair_dev // row_count
    weights = lax.dynamic_slice_in_dim(
        pair_weight, col_index * pair_dev + row_index * kernel_share, kernel_share
    ).astype(jnp.float32)
    kernel = weights[:, None] * summed / math.sqrt(NG)
    return (dielectric, kernel)


def solution(mesh):
    return jax.shard_map(
        shards,
        mesh=mesh,
        in_specs=(P("col", "row"), P(), P(), P(), P(), P("row", "col")),
        out_specs=(P("row", "col"), P(("col", "row"), None)),
        check_vma=False,
    )
```

profile of v0, /device:TPU:0, one launch (start us, length us, event | category | flops | bytes accessed | tf_op | source)
XLA Modules:
  0.0 656.9 jit_solution(1160271850657053020)
XLA Ops:
  7.2 0.0 all-gather.3.cloned.1.call-start
  7.2 0.7 select_select_fusion
  7.9 0.1 dynamic_slice.15
  8.0 2.4 multiply_convert_fusion
  10.4 0.0 all-gather.3.cloned.1.call-update
  10.4 0.0 all-gather.5.cloned.1.call-start
  10.5 18.7 %all_to_all.35 = bf16[4,64,2048]{2,1,0:T(8,128)(2,1)S(1)} all-to-all(bf16[4,64,2048]{2,1,0:T(8,128)(2,1)} %bitcast.38), channel_id=1, replica_groups=mesh['row'=4,'col'=8] {'row'}, dimensions={0} | all-to-all | bytes 2097152 | tf_op jit(solution)/shard_map/all_to_all | solution.py:41
  29.2 0.8 copy.14
  30.0 0.0 copy-start.2
  30.0 0.3 all_to_all.29
  30.3 0.6 copy.15
  30.9 51.7 %all_to_all.36 = bf16[64,8,1024]{2,0,1:T(8,128)(2,1)} all-to-all(bf16[64,8,1024]{2,0,1:T(8,128)(2,1)S(1)} %copy.15), channel_id=1, replica_groups=mesh['row'=4,'col'=8] {'col'}, dimensions={1} | all-to-all | bytes 2097152 | tf_op jit(solution)/shard_map/all_to_all | solution.py:40
  82.5 0.0 all-gather.5.cloned.1.call-update
  82.6 0.6 all-reduce.7.cloned.1.call-start
  83.2 0.0 copy-done.2
  83.2 3.1 gather_fusion.1
  86.4 72.6 %all-gather.3.cloned.1.call-done = bf16[2048,2048]{1,0:T(8,128)(2,1)} async-done(((bf16[256,2048]{1,0:T(8,128)(2,1)}), bf16[2048,2048]{1,0:T(8,128)(2,1)}) %all-gather.3.cloned.1.call-update) | async-done | bytes 8388624 | tf_op jit(solution)/shard_map/all_gather | solution.py:39
  159.0 9.7 %gather_fusion = bf16[512,2048]{1,0:T(8,128)(2,1)} fusion(bf16[2048,2048]{1,0:T(8,128)(2,1)} %all-gather.3.cloned.1.call-done, s32[1024]{0:T(1024)S(1)} %pad_clamp_fusion), kind=kCustom, calls=%fused_computation | custom fusion | bytes 4196352 | tf_op jit(solution)/shard_map/gather | solution.py:65
  168.7 2.9 copy.16
  171.6 2.6 convert_element_type.25
  174.1 8.5 %copy.13 = bf16[8,4,64,2048]{3,2,0,1:T(8,128)(2,1)} copy(bf16[8,4,64,2048]{3,2,1,0:T(8,128)(2,1)} %bitcast.37) | data formatting | bytes 16777216 | tf_op jit(solution)/shard_map/reshape | solution.py:48
  182.6 5.2 fusion
  187.8 0.7 multiply_add_fusion
  188.5 4.8 all-gather.5.cloned.1.call-done
  193.2 15.4 %select_add_fusion = f32[2048,1024]{1,0:T(8,128)S(1)} fusion(f32[2048,1024]{1,0:T(8,128)} %param.11, bf16[2048,2048]{1,0:T(8,128)(2,1)} %bitcast.39, bf16[2048,1024]{1,0:T(8,128)(2,1)} %all-gather.5.cloned.1.call-done, f32[2048]{0:T(1024)S(1)} %get-tuple-element.13, s32[1024]{0:T(1024)S(1)} %iota_add_fusion.1, s32[2048]{0:T(1024)S(1)} %iota_add_fusion), kind=kOutput, calls=%fused_computation.4 | convolution fusion | flops 8600420352 | bytes 29380608 | tf_op jit(solution)/shard_map/dot_general | solution.py:22
  208.6 0.0 copy-start.5
  208.6 0.0 copy-start
  208.6 16.1 %fusion.10 = f32[1024,512]{1,0:T(8,128)} fusion(f32[2048,1024]{1,0:T(8,128)S(1)} %select_add_fusion, bf16[512,2048]{0,1:T(8,128)(2,1)S(1)} %copy.16, f32[2048]{0:T(1024)S(1)} %get-tuple-element.12, f32[512]{0:T(512)S(1)} %gather_fusion.1), kind=kOutput, calls=%fused_computation.16 | convolution fusion | flops 12888047616 | bytes 12593152 | tf_op jit(solution)/shard_map/dot_general | solution.py:86
  224.8 0.0 copy-done.5
  224.8 0.0 copy-done
  224.8 1.6 fusion.12
  226.3 0.0 all-reduce.7.cloned.1.call-update
  226.4 0.0 all-reduce.5.cloned.1.call-start
  226.4 5.9 psum.36
  232.3 79.7 %all-reduce.7.cloned.1.call-done = (f32[1024,512]{1,0:T(8,128)}, f32[1024,512]{1,0:T(8,128)}) async-done(((f32[1024,512]{1,0:T(8,128)}, f32[1024,512]{1,0:T(8,128)}), (f32[1024,512]{1,0:T(8,128)}, f32[1024,512]{1,0:T(8,128)})) %all-reduce.7.cloned.1.call-update) | async-done | bytes 4194320 | tf_op jit(solution)/shard_map/psum | solution.py:14
  312.0 0.0 copy-start.3
  312.0 0.0 copy-start.4
  312.0 0.0 copy-start.6
  312.0 18.0 %fusion.30 = f32[2048,512]{1,0:T(8,128)} fusion(f32[2048,1024]{1,0:T(8,128)} %copy-done.5, f32[1024,512]{1,0:T(8,128)} %get-tuple-element.10, f32[1024]{0:T(1024)S(1)} %psum.36), kind=kOutput, calls=%fused_computation.37 | convolution fusion | flops 12885426176 | bytes 14684160 | tf_op jit(solution)/shard_map/dot_general | solution.py:83
  330.0 0.0 copy-done.3
  330.0 0.0 copy-done.4
  330.0 0.0 copy-done.6
  330.0 15.5 %fusion.15 = f32[2048,512]{1,0:T(8,128)} fusion(f32[2048,1024]{1,0:T(8,128)S(1)} %copy-done.6, f32[1024,512]{1,0:T(8,128)S(1)} %copy-done.3, f32[1024,512]{1,0:T(8,128)S(1)} %copy-done.4, f32[1024]{0:T(1024)S(1)} %psum.36), kind=kOutput, calls=%fused_computation.22 | convolution fusion | flops 12887523328 | bytes 16781312 | tf_op jit(solution)/shard_map/dot_general | solution.py:83
  345.5 0.0 copy-start.1
  345.5 0.0 all-reduce.5.cloned.1.call-update
  345.5 0.3 reduce-scatter.4.cloned.1.call-start
  345.8 270.0 %all-reduce.5.cloned.1.call-done = (f32[2048,512]{1,0:T(8,128)}, f32[2048,512]{1,0:T(8,128)}) async-done(((f32[2048,512]{1,0:T(8,128)}, f32[2048,512]{1,0:T(8,128)}), (f32[2048,512]{1,0:T(8,128)}, f32[2048,512]{1,0:T(8,128)})) %all-reduce.5.cloned.1.call-update) | async-done | bytes 8388624 | tf_op jit(solution)/shard_map/psum | solution.py:82
  615.9 0.0 copy-done.1
  615.9 9.4 %fusion.25 = f32[256,512]{0,1:T(8,128)} fusion(bf16[256,2048]{1,0:T(8,128)(2,1)S(1)} %copy-done.1, f32[2048,512]{1,0:T(8,128)} %get-tuple-element.8, f32[2048,512]{1,0:T(8,128)} %get-tuple-element.9, bf16[512,2048]{0,1:T(8,128)(2,1)S(1)} %copy.16, f32[2048]{0:T(1024)S(1)} %get-tuple-element.12, f32[512]{0:T(512)S(1)} %gather_fusion.1), kind=kOutput, calls=%fused_computation.33 | convolution fusion | flops 3233808384 | bytes 12068864 | tf_op jit(solution)/shard_map/dot_general | solution.py:92
  625.3 2.0 copy.24
  627.3 0.0 reduce-scatter.4.cloned.1.call-update
  627.4 0.8 dynamic-slice_convert_fusion
  628.1 20.1 %reduce-scatter.4.cloned.1.call-done = f32[64,512]{1,0:T(8,128)} async-done(((f32[256,512]{1,0:T(8,128)}), f32[64,512]{1,0:T(8,128)}) %reduce-scatter.4.cloned.1.call-update) | async-done | bytes 131088
  648.3 1.0 copy.25
  649.3 0.8 copy.17
  (6 shorter events, 0.1 us)
Async XLA Ops:
  7.2 151.8 %all-gather.3.cloned.1.call-start = ((), (), s32[]{:S(2)}) async-start(), calls=%async_computation.3 | async-start | bytes 9437184 | tf_op jit(solution)/shard_map/all_gather | solution.py:39
  10.4 182.8 %all-gather.5.cloned.1.call-start = ((), (), s32[]{:S(2)}) async-start(), calls=%async_computation.4 | async-start | bytes 5242880 | tf_op jit(solution)/shard_map/all_gather | solution.py:50
  30.0 53.2 %copy-start.2 = (s32[512]{0:T(512)S(1)}, s32[512]{0:T(512)}, u32[]{:S(2)}) copy-start(s32[512]{0:T(512)} %param.9) | copy-start | bytes 6148
  82.6 229.5 %all-reduce.7.cloned.1.call-start = ((), (), s32[]{:S(2)}) async-start(), calls=%async_computation.7 | async-start | bytes 8388608 | tf_op jit(solution)/shard_map/psum | solution.py:14
  208.6 16.1 %copy-start.5 = (f32[2048,1024]{1,0:T(8,128)}, f32[2048,1024]{1,0:T(8,128)S(1)}, u32[]{:S(2)}) copy-start(f32[2048,1024]{1,0:T(8,128)S(1)} %select_add_fusion) | copy-start | bytes 25165828
  208.6 16.1 %copy-start = (f32[512,2048]{0,1:T(8,128)S(1)}, f32[512,2048]{0,1:T(8,128)}, u32[]{:S(2)}) copy-start(f32[512,2048]{0,1:T(8,128)} %convert_element_type.25) | copy-start | bytes 12582916
  226.4 389.5 %all-reduce.5.cloned.1.call-start = ((), (), s32[]{:S(2)}) async-start(), calls=%async_computation.6 | async-start | bytes 16777216 | tf_op jit(solution)/shard_map/psum | solution.py:82
  312.0 18.0 %copy-start.3 = (f32[1024,512]{1,0:T(8,128)S(1)}, f32[1024,512]{1,0:T(8,128)}, u32[]{:S(2)}) copy-start(f32[1024,512]{1,0:T(8,128)} %get-tuple-element.10) | copy-start | bytes 6291460
  312.0 18.0 %copy-start.4 = (f32[1024,512]{1,0:T(8,128)S(1)}, f32[1024,512]{1,0:T(8,128)}, u32[]{:S(2)}) copy-start(f32[1024,512]{1,0:T(8,128)} %get-tuple-element.11) | copy-start | bytes 6291460
  312.0 18.0 %copy-start.6 = (f32[2048,1024]{1,0:T(8,128)S(1)}, f32[2048,1024]{1,0:T(8,128)}, u32[]{:S(2)}) copy-start(f32[2048,1024]{1,0:T(8,128)} %copy-done.5) | copy-start | bytes 25165828
  345.5 270.4 %copy-start.1 = (bf16[256,2048]{1,0:T(8,128)(2,1)S(1)}, bf16[256,2048]{1,0:T(8,128)(2,1)}, u32[]{:S(2)}) copy-start(bf16[256,2048]{1,0:T(8,128)(2,1)} %param.6) | copy-start | bytes 3145732
  345.5 302.7 %reduce-scatter.4.cloned.1.call-start = ((), (), s32[]{:S(2)}) async-start(), calls=%async_computation.5 | async-start | bytes 655360
Sparse Core Ops, SparseCore 0:
  10.7 148.2 all-gather.2
  160.6 32.6 all-gather.4
  226.5 85.5 all-reduce.6
  345.6 270.1 all-reduce.4
  627.5 20.7 reduce-scatter.3
where the time goes:
time: 660 us; the launch traced here: 657 us
  waiting for transfers between devices  447 us (68%)
  blocking collectives  76.2 us (12%)
  matrix products  74.4 us (11%)
  local copies, waits for them, and re-layouts  29.8 us (5%)
  between operations  14.2 us (2%)
  other arithmetic  13.9 us (2%)
    psum x1, waiting for transfers between devices, shards(): lax.psum(jnp.dot(dielectric, screen_cols, precision=lax.Precision.HIGHEST...  270 us
    psum x1, waiting for transfers between devices, from_root(): return lax.psum(block, axis)  79.7 us
    all_gather x1, waiting for transfers between devices, shards(): left_all = lax.all_gather(scaled, 'col', axis=0, tiled=True)  72.6 us
    all_to_all x1, blocking collectives, shards(): lax.all_to_all(lax.all_to_all(scaled, 'row', split_axis=0, concat_axis=1,...  51.7 us
    dot_general x2, matrix products, shards(): jnp.dot(dielectric, screen_cols, precision=lax.Precision.HIGHEST)  33.4 us
    unnamed x6, waiting for transfers between devices  20.2 us
    all_to_all x1, blocking collectives, shards(): lax.all_to_all(scaled, 'row', split_axis=0, concat_axis=1, tiled=True)  18.7 us
    dot_general x1, matrix products, shards(): lax.dot_general(dielectric, screen_rows, (((0,), (0,)), ((), ())), precis...  16.1 us
  transfers between devices with their start and end apart: 5, of which 5 were waited for; matrix products, arithmetic and copies ran while one was open for 5% of the time, Pallas kernels for 0%

commit v1 on v0

--- a/solution.py
+++ b/solution.py
@@ -37,12 +37,20 @@
     own_factor = lax.dynamic_slice_in_dim(factor, col_index * pair_dev, pair_dev)
     scaled = (pair_density.astype(jnp.float32) * own_factor[:, None]).astype(jnp.bfloat16)
     left_all = lax.all_gather(scaled, "col", axis=0, tiled=True)
-    relaid = lax.all_to_all(
-        lax.all_to_all(scaled, "row", split_axis=0, concat_axis=1, tiled=True),
-        "col",
-        split_axis=1,
-        concat_axis=0,
-        tiled=True,
+    relaid = jnp.concatenate(
+        lax.all_to_all(
+            jnp.stack(
+                jnp.split(
+                    lax.all_to_all(scaled, "row", split_axis=0, concat_axis=1, tiled=True),
+                    lax.axis_size("col"),
+                    axis=1,
+                )
+            ),
+            "col",
+            0,
+            0,
+        ),
+        axis=0,
     )
     share_rows = pair_dev // row_count
     left_order = left_all.reshape(col_count, row_count, share_rows, row_width)

time: 660 us -> 667 us (1.011)
  no operation moved by 1% of the time
where the time goes in v1:
time: 667 us; the launch traced here: 658 us
  waiting for transfers between devices  449 us (67%)
  blocking collectives  77.7 us (12%)
  matrix products  74.4 us (11%)
  local copies, waits for them, and re-layouts  28.3 us (4%)
  between operations  14.5 us (2%)
  other arithmetic  13.9 us (2%)
    psum x1, waiting for transfers between devices, shards(): lax.psum(jnp.dot(dielectric, screen_cols, precision=lax.Precision.HIGHEST...  270 us
    psum x1, waiting for transfers between devices, from_root(): return lax.psum(block, axis)  79.7 us
    all_gather x1, waiting for transfers between devices, shards(): left_all = lax.all_gather(scaled, 'col', axis=0, tiled=True)  74.1 us
    all_to_all x1, blocking collectives, shards(): lax.all_to_all(jnp.stack(jnp.split(lax.all_to_all(scaled, 'row', split_ax...  53.1 us
    dot_general x2, matrix products, shards(): jnp.dot(dielectric, screen_cols, precision=lax.Precision.HIGHEST)  33.5 us
    unnamed x6, waiting for transfers between devices  20.2 us
    all_to_all x1, blocking collectives, shards(): lax.all_to_all(scaled, 'row', split_axis=0, concat_axis=1, tiled=True)  18.7 us
    dot_general x1, matrix products, shards(): lax.dot_general(dielectric, screen_rows, (((0,), (0,)), ((), ())), precis...  16.1 us
  transfers between devices with their start and end apart: 5, of which 5 were waited for; matrix products, arithmetic and copies ran while one was open for 5% of the time, Pallas kernels for 0%

profile of v1, /device:TPU:0, one launch (start us, length us, event | category | flops | bytes accessed | tf_op | source)
XLA Modules:
  0.0 658.0 jit_solution(15576178308354543782)
XLA Ops:
  7.2 0.0 all-gather.3.cloned.1.call-start
  7.2 0.7 select_select_fusion
  7.9 0.1 dynamic_slice.15
  8.0 2.4 multiply_convert_fusion
  10.4 0.0 all-gather.3.cloned.1.call-update
  10.4 0.0 all-gather.5.cloned.1.call-start
  10.5 18.7 %all_to_all.24 = bf16[4,64,2048]{2,1,0:T(8,128)(2,1)S(1)} all-to-all(bf16[4,64,2048]{2,1,0:T(8,128)(2,1)} %bitcast.70), channel_id=1, replica_groups=mesh['row'=4,'col'=8] {'row'}, dimensions={0} | all-to-all | bytes 2097152 | tf_op jit(solution)/shard_map/all_to_all | solution.py:44
  29.2 0.0 copy-start.2
  29.2 0.1 copy.24
  29.4 53.1 %all_to_all.25 = bf16[8,64,1024]{2,1,0:T(8,128)(2,1)} all-to-all(bf16[8,64,1024]{2,1,0:T(8,128)(2,1)S(1)} %fusion.31), channel_id=1, replica_groups=mesh['row'=4,'col'=8] {'col'}, dimensions={0} | all-to-all | bytes 2097152 | tf_op jit(solution)/shard_map/all_to_all | solution.py:41
  82.5 0.0 all-gather.5.cloned.1.call-update
  82.6 0.0 all-reduce.7.cloned.1.call-start
  82.6 0.0 copy-done.2
  82.7 3.1 gather_fusion.1
  85.9 74.1 %all-gather.3.cloned.1.call-done = bf16[2048,2048]{1,0:T(8,128)(2,1)} async-done(((bf16[256,2048]{1,0:T(8,128)(2,1)}), bf16[2048,2048]{1,0:T(8,128)(2,1)}) %all-gather.3.cloned.1.call-update) | async-done | bytes 8388624 | tf_op jit(solution)/shard_map/all_gather | solution.py:39
  159.9 9.7 %gather_fusion = bf16[512,2048]{1,0:T(8,128)(2,1)} fusion(bf16[2048,2048]{1,0:T(8,128)(2,1)} %all-gather.3.cloned.1.call-done, s32[1024]{0:T(1024)S(1)} %pad_clamp_fusion), kind=kCustom, calls=%fused_computation | custom fusion | bytes 4196352 | tf_op jit(solution)/shard_map/gather | solution.py:73
  169.6 2.9 copy.14
  172.5 2.6 convert_element_type.25
  175.1 8.5 %copy.12 = bf16[8,4,64,2048]{3,2,0,1:T(8,128)(2,1)} copy(bf16[8,4,64,2048]{3,2,1,0:T(8,128)(2,1)} %bitcast.69) | data formatting | bytes 16777216 | tf_op jit(solution)/shard_map/reshape | solution.py:56
  183.5 5.2 fusion
  188.7 0.7 multiply_add_fusion
  189.4 4.8 all-gather.5.cloned.1.call-done
  194.2 15.4 %select_add_fusion = f32[2048,1024]{1,0:T(8,128)S(1)} fusion(f32[2048,1024]{1,0:T(8,128)} %param.11, bf16[2048,2048]{1,0:T(8,128)(2,1)} %bitcast.71, bf16[2048,1024]{1,0:T(8,128)(2,1)} %all-gather.5.cloned.1.call-done, f32[2048]{0:T(1024)S(1)} %get-tuple-element.13, s32[1024]{0:T(1024)S(1)} %iota_add_fusion.1, s32[2048]{0:T(1024)S(1)} %iota_add_fusion), kind=kOutput, calls=%fused_computation.4 | convolution fusion | flops 8600420352 | bytes 29380608 | tf_op jit(solution)/shard_map/dot_general | solution.py:22
  209.5 0.0 copy-start.5
  209.6 0.0 copy-start
  209.6 16.1 %fusion.10 = f32[1024,512]{1,0:T(8,128)} fusion(f32[2048,1024]{1,0:T(8,128)S(1)} %select_add_fusion, bf16[512,2048]{0,1:T(8,128)(2,1)S(1)} %copy.14, f32[2048]{0:T(1024)S(1)} %get-tuple-element.12, f32[512]{0:T(512)S(1)} %gather_fusion.1), kind=kOutput, calls=%fused_computation.16 | convolution fusion | flops 12888047616 | bytes 12593152 | tf_op jit(solution)/shard_map/dot_general | solution.py:94
  225.7 0.0 copy-done.5
  225.7 0.0 copy-done
  225.7 1.6 fusion.12
  227.3 0.0 all-reduce.7.cloned.1.call-update
  227.3 0.0 all-reduce.5.cloned.1.call-start
  227.4 5.9 psum.36
  233.3 79.7 %all-reduce.7.cloned.1.call-done = (f32[1024,512]{1,0:T(8,128)}, f32[1024,512]{1,0:T(8,128)}) async-done(((f32[1024,512]{1,0:T(8,128)}, f32[1024,512]{1,0:T(8,128)}), (f32[1024,512]{1,0:T(8,128)}, f32[1024,512]{1,0:T(8,128)})) %all-reduce.7.cloned.1.call-update) | async-done | bytes 4194320 | tf_op jit(solution)/shard_map/psum | solution.py:14
  313.0 0.0 copy-start.3
  313.0 0.0 copy-start.4
  313.0 0.0 copy-start.6
  313.0 18.0 %fusion.30 = f32[2048,512]{1,0:T(8,128)} fusion(f32[2048,1024]{1,0:T(8,128)} %copy-done.5, f32[1024,512]{1,0:T(8,128)} %get-tuple-element.10, f32[1024]{0:T(1024)S(1)} %psum.36), kind=kOutput, calls=%fused_computation.37 | convolution fusion | flops 12885426176 | bytes 14684160 | tf_op jit(solution)/shard_map/dot_general | solution.py:91
  331.0 0.0 copy-done.3
  331.0 0.0 copy-done.4
  331.0 0.0 copy-done.6
  331.0 15.5 %fusion.15 = f32[2048,512]{1,0:T(8,128)} fusion(f32[2048,1024]{1,0:T(8,128)S(1)} %copy-done.6, f32[1024,512]{1,0:T(8,128)S(1)} %copy-done.3, f32[1024,512]{1,0:T(8,128)S(1)} %copy-done.4, f32[1024]{0:T(1024)S(1)} %psum.36), kind=kOutput, calls=%fused_computation.22 | convolution fusion | flops 12887523328 | bytes 16781312 | tf_op jit(solution)/shard_map/dot_general | solution.py:91
  346.4 0.0 copy-start.1
  346.4 0.0 all-reduce.5.cloned.1.call-update
  346.5 0.3 reduce-scatter.4.cloned.1.call-start
  346.8 270.0 %all-reduce.5.cloned.1.call-done = (f32[2048,512]{1,0:T(8,128)}, f32[2048,512]{1,0:T(8,128)}) async-done(((f32[2048,512]{1,0:T(8,128)}, f32[2048,512]{1,0:T(8,128)}), (f32[2048,512]{1,0:T(8,128)}, f32[2048,512]{1,0:T(8,128)})) %all-reduce.5.cloned.1.call-update) | async-done | bytes 8388624 | tf_op jit(solution)/shard_map/psum | solution.py:90
  616.8 0.0 copy-done.1
  616.8 9.4 %fusion.25 = f32[256,512]{0,1:T(8,128)} fusion(bf16[256,2048]{1,0:T(8,128)(2,1)S(1)} %copy-done.1, f32[2048,512]{1,0:T(8,128)} %get-tuple-element.8, f32[2048,512]{1,0:T(8,128)} %get-tuple-element.9, bf16[512,2048]{0,1:T(8,128)(2,1)S(1)} %copy.14, f32[2048]{0:T(1024)S(1)} %get-tuple-element.12, f32[512]{0:T(512)S(1)} %gather_fusion.1), kind=kOutput, calls=%fused_computation.33 | convolution fusion | flops 3233808384 | bytes 12068864 | tf_op jit(solution)/shard_map/dot_general | solution.py:100
  626.2 2.0 copy.22
  628.2 0.0 reduce-scatter.4.cloned.1.call-update
  628.3 0.8 dynamic-slice_convert_fusion
  629.0 20.1 %reduce-scatter.4.cloned.1.call-done = f32[64,512]{1,0:T(8,128)} async-done(((f32[256,512]{1,0:T(8,128)}), f32[64,512]{1,0:T(8,128)}) %reduce-scatter.4.cloned.1.call-update) | async-done | bytes 131088
  649.2 1.0 copy.23
  650.2 0.8 copy.15
  (14 shorter events, 0.2 us)
Async XLA Ops:
  7.2 152.8 %all-gather.3.cloned.1.call-start = ((), (), s32[]{:S(2)}) async-start(), calls=%async_computation.3 | async-start | bytes 9437184 | tf_op jit(solution)/shard_map/all_gather | solution.py:39
  10.4 183.7 %all-gather.5.cloned.1.call-start = ((), (), s32[]{:S(2)}) async-start(), calls=%async_computation.4 | async-start | bytes 5242880 | tf_op jit(solution)/shard_map/all_gather | solution.py:58
  29.2 53.5 %copy-start.2 = (s32[512]{0:T(512)S(1)}, s32[512]{0:T(512)}, u32[]{:S(2)}) copy-start(s32[512]{0:T(512)} %param.9) | copy-start | bytes 6148
  82.6 230.4 %all-reduce.7.cloned.1.call-start = ((), (), s32[]{:S(2)}) async-start(), calls=%async_computation.7 | async-start | bytes 8388608 | tf_op jit(solution)/shard_map/psum | solution.py:14
  209.5 16.1 %copy-start.5 = (f32[2048,1024]{1,0:T(8,128)}, f32[2048,1024]{1,0:T(8,128)S(1)}, u32[]{:S(2)}) copy-start(f32[2048,1024]{1,0:T(8,128)S(1)} %select_add_fusion) | copy-start | bytes 25165828
  209.6 16.1 %copy-start = (f32[512,2048]{0,1:T(8,128)S(1)}, f32[512,2048]{0,1:T(8,128)}, u32[]{:S(2)}) copy-start(f32[512,2048]{0,1:T(8,128)} %convert_element_type.25) | copy-start | bytes 12582916
  227.3 389.5 %all-reduce.5.cloned.1.call-start = ((), (), s32[]{:S(2)}) async-start(), calls=%async_computation.6 | async-start | bytes 16777216 | tf_op jit(solution)/shard_map/psum | solution.py:90
  313.0 18.0 %copy-start.3 = (f32[1024,512]{1,0:T(8,128)S(1)}, f32[1024,512]{1,0:T(8,128)}, u32[]{:S(2)}) copy-start(f32[1024,512]{1,0:T(8,128)} %get-tuple-element.10) | copy-start | bytes 6291460
  313.0 18.0 %copy-start.4 = (f32[1024,512]{1,0:T(8,128)S(1)}, f32[1024,512]{1,0:T(8,128)}, u32[]{:S(2)}) copy-start(f32[1024,512]{1,0:T(8,128)} %get-tuple-element.11) | copy-start | bytes 6291460
  313.0 18.0 %copy-start.6 = (f32[2048,1024]{1,0:T(8,128)S(1)}, f32[2048,1024]{1,0:T(8,128)}, u32[]{:S(2)}) copy-start(f32[2048,1024]{1,0:T(8,128)} %copy-done.5) | copy-start | bytes 25165828
  346.4 270.3 %copy-start.1 = (bf16[256,2048]{1,0:T(8,128)(2,1)S(1)}, bf16[256,2048]{1,0:T(8,128)(2,1)}, u32[]{:S(2)}) copy-start(bf16[256,2048]{1,0:T(8,128)(2,1)} %param.6) | copy-start | bytes 3145732
  346.5 302.7 %reduce-scatter.4.cloned.1.call-start = ((), (), s32[]{:S(2)}) async-start(), calls=%async_computation.5 | async-start | bytes 655360
Sparse Core Ops, SparseCore 0:
  10.7 149.2 all-gather.2
  161.5 32.6 all-gather.4
  227.4 85.5 all-reduce.6
  346.6 270.1 all-reduce.4
  628.4 20.7 reduce-scatter.3
